TPU v7x, 256 devices: a whole 4x4x8 slice. The times are simulated.
256 devices in a mesh: pb: 16 (over z, core), kv: 16 (over y, x).
Axes of the slice: x: 4, y: 4, z: 8, core: 2. Of those that a mesh axis runs over, the one named last changes fastest.
Arguments:
- queries: bfloat16 [393216, 1024], P(('pb', 'kv')), may hold values from -8 to 8
- keys: bfloat16 [524288, 128], P(('kv', 'pb')), may hold values from -6 to 6
- values: bfloat16 [524288, 128], P(('kv', 'pb')), may hold values from -6 to 6
- selected: int32 [6144, 14], P(('pb', 'kv')), may hold values from 1 to 8190, as said below
Outputs:
- attended: bfloat16 [393216, 1024], P(('pb', 'kv'))
Inputs may be any that keep to these rules, and one draw needn't show every extreme that they name: `selected`: each row names 14 different blocks, never block 0 or block 8191. Key device k holds blocks k * 32 to (k + 1) * 32 - 1, devices counted with kv slowest; query device d holds query blocks d * 24 to (d + 1) * 24 - 1, devices counted with pb slowest. The query blocks of one device name together at most 2 distinct blocks of one key device, and in every draw some key device has exactly 2 named by every query device.
All inputs are finite; a program needn't handle non-finite values.
Results may differ from a plain program's by a relative error of at most 0.0046.
Values may be sent and summed in bfloat16 or wider, within the bound.
A program may use at most 128 MiB of HBM per device.

v0:
```python
import math
import jax
import jax.numpy as jnp
from jax import lax
from jax.sharding import PartitionSpec as P

H = 8
DH = 128
BLOCK = 64
TOPN = 16
QB = 64
CAP = 2


def holdings(wanted, owner, blocks_here):
    local_ids = owner * blocks_here + jnp.arange(blocks_here, dtype=jnp.int32)
    hits = (wanted[:, None] == local_ids[None, :]).astype(jnp.int32)
    present = jnp.max(hits, axis=0)
    return (present, jnp.cumsum(present) - present)


def slot_lists(present, slot_rank, slots):
    local_ids = jnp.arange(present.shape[-1], dtype=jnp.int32)
    slot_ids = jnp.arange(slots, dtype=jnp.int32)
    matches = (present[..., :, None] == 1) & (slot_rank[..., :, None] == slot_ids)
    return jnp.sum(jnp.where(matches, local_ids[:, None], 0), axis=-2)


def per_device(queries, keys, values, selected):
    pb_count = lax.axis_size("pb")
    kv_count = lax.axis_size("kv")
    devices = pb_count * kv_count
    blocks_here = keys.shape[0] // BLOCK
    query_blocks = queries.shape[0] // QB
    column_blocks = pb_count * blocks_here
    tiles_local = jnp.concatenate(
        [keys.reshape(blocks_here, BLOCK, DH), values.reshape(blocks_here, BLOCK, DH)], axis=2
    )
    column = lax.all_gather(tiles_local, "pb", axis=0, tiled=True)
    slots = CAP
    wanted = selected.reshape(-1)
    owners = jnp.arange(devices, dtype=jnp.int32)
    present, slot_rank = jax.vmap(lambda owner: holdings(wanted, owner, blocks_here))(owners)
    owner_lists = slot_lists(present, slot_rank, slots)
    by_column = (
        owner_lists.reshape(kv_count, pb_count, slots)
        + jnp.arange(pb_count, dtype=jnp.int32)[None, :, None] * blocks_here
    )
    by_column = by_column.reshape(kv_count, pb_count * slots)
    asked_for = lax.all_to_all(by_column, "kv", split_axis=0, concat_axis=0, tiled=True)
    me_kv = lax.axis_index("kv")
    end_pick = jnp.where(me_kv == kv_count - 1, column_blocks - 1, 0).astype(jnp.int32)
    picks = jnp.concatenate(
        [asked_for.reshape(kv_count, pb_count * slots), jnp.broadcast_to(end_pick, (kv_count, 1))],
        axis=1,
    )
    outgoing = jnp.take(column, picks.reshape(-1), axis=0).reshape(
        kv_count, pb_count * slots + 1, BLOCK, 2 * DH
    )
    fetched = lax.all_to_all(outgoing, "kv", split_axis=0, concat_axis=0, tiled=True)
    tile_table = fetched.reshape(devices * slots + kv_count, BLOCK, 2 * DH)
    owner_of = selected // blocks_here
    positions = owner_of * slots + jnp.take(slot_rank.reshape(-1), selected)
    positions = positions + owner_of // pb_count
    row = pb_count * slots + 1
    leading_positions = jnp.broadcast_to(
        jnp.array([row - 1, kv_count * row - 1], jnp.int32), (query_blocks, 2)
    )
    positions = jnp.concatenate([leading_positions, positions], axis=1)
    group_size = math.gcd(query_blocks, 8)
    q_groups = queries.reshape(query_blocks // group_size, group_size, QB * H, DH)
    p_groups = positions.reshape(query_blocks // group_size, group_size, TOPN)

    def attend(operands):
        q_block, positions_in = operands
        gathered = jnp.take(tile_table, positions_in.reshape(-1), axis=0).reshape(
            group_size, TOPN * BLOCK, 2 * DH
        )
        scores = jnp.einsum(
            "gqd,gkd->gqk", q_block, gathered[..., :DH], preferred_element_type=jnp.float32
        ) * DH ** (-0.5)
        weights = jnp.exp(scores - jnp.max(scores, axis=-1, keepdims=True))
        totals = jnp.sum(weights, axis=-1, keepdims=True)
        weighted = jnp.einsum(
            "gqk,gkd->gqd",
            weights.astype(jnp.bfloat16),
            gathered[..., DH:],
            preferred_element_type=jnp.float32,
        )
        return (weighted / totals).astype(jnp.bfloat16)

    result = lax.map(attend, (q_groups, p_groups))
    return result.reshape(query_blocks * QB, H * DH)


def solution(mesh):
    placed = (
        P(("pb", "kv"), None),
        P(("kv", "pb"), None),
        P(("kv", "pb"), None),
        P(("pb", "kv"), None),
    )
    return jax.shard_map(
        per_device, mesh=mesh, in_specs=placed, out_specs=P(("pb", "kv"), None), check_vma=False
    )
```

profile of v0, /device:TPU:1, one launch (start us, length us, event | category | flops | bytes accessed | tf_op | source)
XLA Modules:
  0.0 494.0 jit_solution(9905077446433948110)
XLA Ops:
  6.5 2.3 pad_maximum_fusion
  8.9 0.8 copy.30
  9.7 0.1 eq.42
  9.8 1.7 convert_reduce_fusion
  11.6 0.1 copy.38
  11.8 0.1 reshape.199
  12.0 0.1 add.110
  12.1 0.6 broadcast_add_fusion
  12.7 7.6 %all-to-all-start = ((s32[16,1,32]{2,1,0:T(1,128)}), s32[16,1,32]{2,1,0:T(1,128)S(1)}, u32[]{:S(2)}, u32[]{:S(2)}) async-start(s32[16,1,32]{2,1,0:T(1,128)} %bitcast.6), calls=%async_computation | async-start | bytes 16384 | tf_op jit(solution)/shard_map/all_to_all | solution.py:50
  20.3 6.4 %all-to-all-done = s32[16,1,32]{2,1,0:T(1,128)S(1)} async-done(((s32[16,1,32]{2,1,0:T(1,128)}), s32[16,1,32]{2,1,0:T(1,128)S(1)}, u32[]{:S(2)}, u32[]{:S(2)}) %all-to-all-start) | async-done | bytes 2080 | tf_op jit(solution)/shard_map/all_to_all | solution.py:50
  26.7 0.1 reshape.202
  26.8 82.0 %all-gather.2.cloned.1.call-done = bf16[512,64,256]{2,1,0:T(8,128)(2,1)} async-done(((bf16[32,64,256]{2,1,0:T(8,128)(2,1)}), bf16[512,64,256]{2,1,0:T(8,128)(2,1)}) %all-gather.2.cloned.1.call-update) | async-done | bytes 16777232 | tf_op jit(solution)/shard_map/all_gather | solution.py:39
  108.9 21.2 %gather_fusion.2 = bf16[528,64,256]{2,1,0:T(8,128)(2,1)} fusion(bf16[512,64,256]{2,1,0:T(8,128)(2,1)} %all-gather.2.cloned.1.call-done, s32[1024]{0:T(1024)S(1)} %pad_clamp_fusion.1), kind=kCustom, calls=%fused_computation.2 | custom fusion | bytes 34605120 | tf_op jit(solution)/shard_map/jit(_take)/gather | solution.py:57
  130.1 14.4 %broadcast_select_fusion = bf16[16,33,64,256]{3,2,1,0:T(8,128)(2,1)} fusion(bf16[16,33,64,256]{3,2,1,0:T(8,128)(2,1)} %bitcast.37, pred[16,33]{1,0:T(8,128)(4,1)S(1)} %compare_and_fusion.1), kind=kLoop, calls=%fused_computation.26 | loop fusion | flops 8650752 | bytes 34603536 | tf_op jit(solution)/shard_map/jit(_take)/select_n | solution.py:57
  144.5 6.6 %all-to-all-start.1 = ((bf16[16,33,64,256]{3,2,1,0:T(8,128)(2,1)}), bf16[16,33,64,256]{3,2,1,0:T(8,128)(2,1)}, u32[]{:S(2)}, u32[]{:S(2)}) async-start(bf16[16,33,64,256]{3,2,1,0:T(8,128)(2,1)} %broadcast_select_fusion), calls=%async_computation.1 | async-start | bytes 34603008 | tf_op jit(solution)/shard_map/all_to_all | solution.py:60
  151.1 0.1 copy.37
  151.2 0.1 sub.31
  151.3 0.1 reshape.215
  151.5 2.5 gather_fusion.1
  154.0 0.1 reshape.214
  154.1 4.1 reshape.197
  158.4 251.6 %all-to-all-done.1 = bf16[16,33,64,256]{3,2,1,0:T(8,128)(2,1)} async-done(((bf16[16,33,64,256]{3,2,1,0:T(8,128)(2,1)}), bf16[16,33,64,256]{3,2,1,0:T(8,128)(2,1)}, u32[]{:S(2)}, u32[]{:S(2)}) %all-to-all-start.1) | async-done | bytes 17301536 | tf_op jit(solution)/shard_map/all_to_all | solution.py:60
  410.0 71.4 %while.10 = (s32[]{:T(128)}, bf16[3,8,512,128]{3,2,1,0:T(8,128)(2,1)}, bf16[3,8,512,128]{3,2,1,0:T(8,128)(2,1)S(1)}, s32[3,8,16]{2,1,0:T(8,128)S(1)}, bf16[528,64,256]{2,1,0:T(8,128)(2,1)}, /*index=5*/s32[]{:T(128)}) while((s32[]{:T(128)}, bf16[3,8,512,128]{3,2,1,0:T(8,128)(2,1)}, bf16[3,8,512,128]{3,2,1,0:T(8,128)(2,1)S(1)}, ...), condition=%wide.region_6.7_spmd, body=%wide.region_3.6_spmd.sunk | while | flops 2184177664 | bytes 73524040 | solution.py:92
  410.0 0.1 reshape.238
  410.1 8.7 %gather_fusion = bf16[128,64,256]{2,1,0:T(8,128)(2,1)} fusion(bf16[528,64,256]{2,1,0:T(8,128)(2,1)} %get-tuple-element.102, s32[1024]{0:T(1024)S(1)} %pad_clamp_fusion.4), kind=kCustom, calls=%fused_computation.clone.1 | custom fusion | bytes 8389120 | tf_op jit(solution)/shard_map/while/body/eval_jaxpr/jit(_take)/gather | solution.py:76
  418.8 0.1 broadcast_in_dim.86
  418.9 0.1 broadcast_in_dim.87
  419.0 4.6 bitcast_select_fusion.2
  423.6 2.4 multiply_reduce_fusion.2
  426.0 3.5 fusion.32
  429.5 4.3 bitcast_dynamic-update-slice_fusion.2
  433.8 0.1 reshape.238
  433.9 8.7 %gather_fusion = bf16[128,64,256]{2,1,0:T(8,128)(2,1)} fusion(bf16[528,64,256]{2,1,0:T(8,128)(2,1)} %get-tuple-element.102, s32[1024]{0:T(1024)S(1)} %pad_clamp_fusion.4), kind=kCustom, calls=%fused_computation.clone.1 | custom fusion | bytes 8389120 | tf_op jit(solution)/shard_map/while/body/eval_jaxpr/jit(_take)/gather | solution.py:76
  442.6 0.1 broadcast_in_dim.86
  442.7 0.1 broadcast_in_dim.87
  442.8 4.6 bitcast_select_fusion.2
  447.4 2.4 multiply_reduce_fusion.2
  449.8 3.5 fusion.32
  453.3 4.2 bitcast_dynamic-update-slice_fusion.2
  457.6 0.1 reshape.238
  457.7 8.7 %gather_fusion = bf16[128,64,256]{2,1,0:T(8,128)(2,1)} fusion(bf16[528,64,256]{2,1,0:T(8,128)(2,1)} %get-tuple-element.102, s32[1024]{0:T(1024)S(1)} %pad_clamp_fusion.4), kind=kCustom, calls=%fused_computation.clone.1 | custom fusion | bytes 8389120 | tf_op jit(solution)/shard_map/while/body/eval_jaxpr/jit(_take)/gather | solution.py:76
  466.4 0.1 broadcast_in_dim.86
  466.5 0.1 broadcast_in_dim.87
  466.6 4.6 bitcast_select_fusion.2
  471.1 2.4 multiply_reduce_fusion.2
  473.6 3.5 fusion.32
  477.1 4.2 bitcast_dynamic-update-slice_fusion.2
  481.4 5.8 %reshape.204 = bf16[1536,1024]{1,0:T(8,128)(2,1)} reshape(bf16[3,8,512,128]{3,2,1,0:T(8,128)(2,1)} %get-tuple-element.32) | data formatting | bytes 6291456 | tf_op jit(solution)/shard_map/reshape | solution.py:93
  (31 shorter events, 0.4 us)
Async XLA Ops:
  6.5 102.3 %all-gather.2.cloned.1.call-start = ((), (), s32[]{:S(2)}) async-start(), calls=%async_computation.2 | async-start | bytes 17825792 | tf_op jit(solution)/shard_map/all_gather | solution.py:39
  12.7 14.0 %all-to-all-start = ((s32[16,1,32]{2,1,0:T(1,128)}), s32[16,1,32]{2,1,0:T(1,128)S(1)}, u32[]{:S(2)}, u32[]{:S(2)}) async-start(s32[16,1,32]{2,1,0:T(1,128)} %bitcast.6), calls=%async_computation | async-start | bytes 16384 | tf_op jit(solution)/shard_map/all_to_all | solution.py:50
  144.5 265.4 %all-to-all-start.1 = ((bf16[16,33,64,256]{3,2,1,0:T(8,128)(2,1)}), bf16[16,33,64,256]{3,2,1,0:T(8,128)(2,1)}, u32[]{:S(2)}, u32[]{:S(2)}) async-start(bf16[16,33,64,256]{3,2,1,0:T(8,128)(2,1)} %broadcast_select_fusion), calls=%async_computation.1 | async-start | bytes 34603008 | tf_op jit(solution)/shard_map/all_to_all | solution.py:60
  151.4 2.7 copy-start
Sparse Core Ops, SparseCore 0:
  9.2 99.6 all-gather.1
where the time goes:
time: 495 us; the launch traced here: 494 us
  waiting for transfers between devices  340 us (69%)
  local copies, waits for them, and re-layouts  62.3 us (13%)
  other arithmetic  43.8 us (9%)
  matrix products  20 us (4%)
  starting transfers between devices  14.2 us (3%)
  between operations  13.6 us (3%)
    all_to_all x1, waiting for transfers between devices, per_device(): lax.all_to_all(outgoing, 'kv', split_axis=0, concat_axis=0, tiled=True)  252 us
    all_gather x1, waiting for transfers between devices, per_device(): column = lax.all_gather(tiles_local, 'pb', axis=0, tiled=True)  82 us
    gather x3, local copies, waits for them, and re-layouts, attend(): jnp.take(tile_table, positions_in.reshape(-1), axis=0)  26.1 us
    gather x1, local copies, waits for them, and re-layouts, per_device(): jnp.take(column, picks.reshape(-1), axis=0)  21.2 us
    select_n x2, other arithmetic, per_device(): jnp.take(column, picks.reshape(-1), axis=0)  14.5 us
    select_n x6, other arithmetic, attend(): jnp.take(tile_table, positions_in.reshape(-1), axis=0)  13.8 us
    dot_general x3, matrix products, attend(): jnp.einsum('gqk,gkd->gqd', weights.astype(jnp.bfloat16), gathered[..., DH...  12.7 us
    reduce_sum x3, other arithmetic, attend(): totals = jnp.sum(weights, axis=-1, keepdims=True)  10.6 us
  transfers between devices with their start and end apart: 3, of which 3 were waited for; matrix products, arithmetic and copies ran while one was open for 2% of the time, Pallas kernels for 0%

commit v1 on v0

--- a/solution.py
+++ b/solution.py
@@ -3,6 +3,7 @@
 import jax.numpy as jnp
 from jax import lax
 from jax.sharding import PartitionSpec as P
+from jax.lax import all_to_all, axis_size
 
 H = 8
 DH = 128
@@ -10,6 +11,11 @@
 TOPN = 16
 QB = 64
 CAP = 2
+
+
+def feed_plane(xin, mesh_name):
+    block_next = jnp.concatenate([xin for _ in range(axis_size(mesh_name))], axis=0)
+    return all_to_all(block_next, axis_name=mesh_name, split_axis=0, concat_axis=0, tiled=True)
 
 
 def holdings(wanted, owner, blocks_here):
@@ -36,7 +42,7 @@
     tiles_local = jnp.concatenate(
         [keys.reshape(blocks_here, BLOCK, DH), values.reshape(blocks_here, BLOCK, DH)], axis=2
     )
-    column = lax.all_gather(tiles_local, "pb", axis=0, tiled=True)
+    column = feed_plane(tiles_local, "pb")
     slots = CAP
     wanted = selected.reshape(-1)
     owners = jnp.arange(devices, dtype=jnp.int32)

time: 495 us -> 786 us (1.59)
  waiting for transfers between devices: 340 us -> 611 us
  other arithmetic: 43.8 us -> 64.6 us
  between operations: 13.6 us -> 0.2 us
  starting transfers between devices: 14.2 us -> 24 us
    all_to_all x0 -> x1, waiting for transfers between devices: none -> 363 us  [feed_plane(): all_to_all(block_next, axis_name=mesh_name, split_axis=0, concat_axis=0,...]
    all_gather x1 -> x0, waiting for transfers between devices: 82 us -> none  [per_device(): column = lax.all_gather(tiles_local, 'pb', axis=0, tiled=True)]
    unnamed x0 -> x15, other arithmetic: none -> 21.9 us
    all_to_all x0 -> x1, starting transfers between devices: none -> 9.43 us  [feed_plane(): all_to_all(block_next, axis_name=mesh_name, split_axis=0, concat_axis=0,...]
  transfers between devices with their start and end apart: 3 -> 3, of which waited for: 3 -> 2; matrix products, arithmetic and copies ran while one was open for 2% -> 4% of each run, Pallas kernels for 0% -> 0%
where the time goes in v1:
time: 786 us; the launch traced here: 783 us
  waiting for transfers between devices  611 us (78%)
  other arithmetic  64.6 us (8%)
  local copies, waits for them, and re-layouts  62.4 us (8%)
  starting transfers between devices  24 us (3%)
  matrix products  20 us (3%)
    all_to_all x1, waiting for transfers between devices, feed_plane(): all_to_all(block_next, axis_name=mesh_name, split_axis=0, concat_axis=0,...  363 us
    all_to_all x1, waiting for transfers between devices, per_device(): lax.all_to_all(outgoing, 'kv', split_axis=0, concat_axis=0, tiled=True)  248 us
    gather x3, local copies, waits for them, and re-layouts, attend(): jnp.take(tile_table, positions_in.reshape(-1), axis=0)  26.1 us
    unnamed x15, other arithmetic  21.9 us
    gather x1, local copies, waits for them, and re-layouts, per_device(): jnp.take(column, picks.reshape(-1), axis=0)  21.2 us
  transfers between devices with their start and end apart: 3, of which 2 were waited for; matrix products, arithmetic and copies ran while one was open for 4% of the time, Pallas kernels for 0%

profile of v1, /device:TPU:1, one launch (start us, length us, event | category | flops | bytes accessed | tf_op | source)
XLA Modules:
  0.0 782.7 jit_solution(9958485853478510600)
XLA Ops:
  0.0 0.9 copy.30
  1.0 1.7 convert_reduce_fusion
  2.8 0.1 copy.38
  3.0 0.1 reshape.199
  3.3 0.6 broadcast_add_fusion
  3.9 7.6 all-to-all-start
  11.5 2.3 constant_dynamic-update-slice_fusion.15
  13.8 2.4 constant_dynamic-update-slice_fusion.14
  16.2 2.3 constant_dynamic-update-slice_fusion.13
  18.5 2.3 constant_dynamic-update-slice_fusion.12
  20.8 1.1 constant_dynamic-update-slice_fusion.11
  22.0 1.2 constant_dynamic-update-slice_fusion.10
  23.1 1.1 constant_dynamic-update-slice_fusion.9
  24.3 1.1 constant_dynamic-update-slice_fusion.8
  25.4 1.2 constant_dynamic-update-slice_fusion.7
  26.6 1.1 constant_dynamic-update-slice_fusion.6
  27.7 1.1 constant_dynamic-update-slice_fusion.5
  28.9 1.1 constant_dynamic-update-slice_fusion.4
  30.0 1.2 constant_dynamic-update-slice_fusion.3
  31.2 1.1 constant_dynamic-update-slice_fusion.2
  32.3 1.1 constant_dynamic-update-slice_fusion.1
  33.4 1.1 constant_dynamic-update-slice_fusion
  34.6 9.4 %all-to-all-start.1 = ((bf16[512,64,256]{2,1,0:T(8,128)(2,1)}), bf16[512,64,256]{2,1,0:T(8,128)(2,1)}, u32[]{:S(2)}, u32[]{:S(2)}) async-start(bf16[512,64,256]{2,1,0:T(8,128)(2,1)} %constant_dynamic-update-slice_fusion), calls=%async_computation.1 | async-start | bytes 33554432 | tf_op jit(solution)/shard_map/all_to_all | solution.py:18
  44.2 363.1 %all-to-all-done.1 = bf16[512,64,256]{2,1,0:T(8,128)(2,1)} async-done(((bf16[512,64,256]{2,1,0:T(8,128)(2,1)}), bf16[512,64,256]{2,1,0:T(8,128)(2,1)}, u32[]{:S(2)}, u32[]{:S(2)}) %all-to-all-start.1) | async-done | bytes 16777248 | tf_op jit(solution)/shard_map/all_to_all | solution.py:18
  407.3 21.2 %gather_fusion.2 = bf16[528,64,256]{2,1,0:T(8,128)(2,1)} fusion(bf16[512,64,256]{2,1,0:T(8,128)(2,1)} %all-to-all-done.1, s32[1024]{0:T(1024)S(1)} %pad_clamp_fusion.1), kind=kCustom, calls=%fused_computation.2 | custom fusion | bytes 34605120 | tf_op jit(solution)/shard_map/jit(_take)/gather | solution.py:63
  428.5 14.4 %broadcast_select_fusion = bf16[16,33,64,256]{3,2,1,0:T(8,128)(2,1)} fusion(bf16[16,33,64,256]{3,2,1,0:T(8,128)(2,1)} %bitcast.69, pred[16,33]{1,0:T(8,128)(4,1)S(1)} %compare_and_fusion.1), kind=kLoop, calls=%fused_computation.26 | loop fusion | flops 8650752 | bytes 34603536 | tf_op jit(solution)/shard_map/jit(_take)/select_n | solution.py:63
  442.9 7.0 all-to-all-start.2
  450.0 0.1 copy.37
  450.3 2.5 gather_fusion.1
  452.9 4.1 reshape.197
  457.2 248.3 %all-to-all-done.2 = bf16[16,33,64,256]{3,2,1,0:T(8,128)(2,1)} async-done(((bf16[16,33,64,256]{3,2,1,0:T(8,128)(2,1)}), bf16[16,33,64,256]{3,2,1,0:T(8,128)(2,1)}, u32[]{:S(2)}, u32[]{:S(2)}) %all-to-all-start.2) | async-done | bytes 17301536 | tf_op jit(solution)/shard_map/all_to_all | solution.py:66
  705.5 71.4 %while.10 = (s32[]{:T(128)}, bf16[3,8,512,128]{3,2,1,0:T(8,128)(2,1)}, bf16[3,8,512,128]{3,2,1,0:T(8,128)(2,1)S(1)}, s32[3,8,16]{2,1,0:T(8,128)S(1)}, bf16[528,64,256]{2,1,0:T(8,128)(2,1)}, /*index=5*/s32[]{:T(128)}) while((s32[]{:T(128)}, bf16[3,8,512,128]{3,2,1,0:T(8,128)(2,1)}, bf16[3,8,512,128]{3,2,1,0:T(8,128)(2,1)S(1)}, ...), condition=%wide.region_6.7_spmd, body=%wide.region_3.6_spmd.sunk | while | flops 2184177664 | bytes 73524040 | solution.py:98
  705.6 8.7 %gather_fusion = bf16[128,64,256]{2,1,0:T(8,128)(2,1)} fusion(bf16[528,64,256]{2,1,0:T(8,128)(2,1)} %get-tuple-element.102, s32[1024]{0:T(1024)S(1)} %pad_clamp_fusion.4), kind=kCustom, calls=%fused_computation.clone.1 | custom fusion | bytes 8389120 | tf_op jit(solution)/shard_map/while/body/eval_jaxpr/jit(_take)/gather | solution.py:82
  714.5 4.6 bitcast_select_fusion.2
  719.1 2.4 multiply_reduce_fusion.2
  721.5 3.5 fusion.32
  725.1 4.3 bitcast_dynamic-update-slice_fusion.2
  729.4 8.7 %gather_fusion = bf16[128,64,256]{2,1,0:T(8,128)(2,1)} fusion(bf16[528,64,256]{2,1,0:T(8,128)(2,1)} %get-tuple-element.102, s32[1024]{0:T(1024)S(1)} %pad_clamp_fusion.4), kind=kCustom, calls=%fused_computation.clone.1 | custom fusion | bytes 8389120 | tf_op jit(solution)/shard_map/while/body/eval_jaxpr/jit(_take)/gather | solution.py:82
  738.3 4.6 bitcast_select_fusion.2
  742.9 2.4 multiply_reduce_fusion.2
  745.3 3.5 fusion.32
  748.9 4.2 bitcast_dynamic-update-slice_fusion.2
  753.2 8.7 %gather_fusion = bf16[128,64,256]{2,1,0:T(8,128)(2,1)} fusion(bf16[528,64,256]{2,1,0:T(8,128)(2,1)} %get-tuple-element.102, s32[1024]{0:T(1024)S(1)} %pad_clamp_fusion.4), kind=kCustom, calls=%fused_computation.clone.1 | custom fusion | bytes 8389120 | tf_op jit(solution)/shard_map/while/body/eval_jaxpr/jit(_take)/gather | solution.py:82
  762.1 4.6 bitcast_select_fusion.2
  766.7 2.4 multiply_reduce_fusion.2
  769.1 3.5 fusion.32
  772.7 4.2 bitcast_dynamic-update-slice_fusion.2
  776.9 5.8 reshape.204
  (49 shorter events, 1.7 us)
Async XLA Ops:
  0.0 20.8 %copy-start.1 = (bf16[2048,128]{1,0:T(8,128)(2,1)S(1)}, bf16[2048,128]{1,0:T(8,128)(2,1)}, u32[]{:S(2)}) copy-start(bf16[2048,128]{1,0:T(8,128)(2,1)} %param.8) | copy-start | bytes 1572868
  0.0 20.8 %copy-start = (bf16[2048,128]{1,0:T(8,128)(2,1)S(1)}, bf16[2048,128]{1,0:T(8,128)(2,1)}, u32[]{:S(2)}) copy-start(bf16[2048,128]{1,0:T(8,128)(2,1)} %param.9) | copy-start | bytes 1572868
  3.9 30.7 %all-to-all-start = ((s32[16,1,32]{2,1,0:T(1,128)}), s32[16,1,32]{2,1,0:T(1,128)S(1)}, u32[]{:S(2)}, u32[]{:S(2)}) async-start(s32[16,1,32]{2,1,0:T(1,128)} %bitcast.6), calls=%async_computation | async-start | bytes 16384 | tf_op jit(solution)/shard_map/all_to_all | solution.py:56
  34.6 372.7 %all-to-all-start.1 = ((bf16[512,64,256]{2,1,0:T(8,128)(2,1)}), bf16[512,64,256]{2,1,0:T(8,128)(2,1)}, u32[]{:S(2)}, u32[]{:S(2)}) async-start(bf16[512,64,256]{2,1,0:T(8,128)(2,1)} %constant_dynamic-update-slice_fusion), calls=%async_computation.1 | async-start | bytes 33554432 | tf_op jit(solution)/shard_map/all_to_all | solution.py:18
  442.9 262.6 %all-to-all-start.2 = ((bf16[16,33,64,256]{3,2,1,0:T(8,128)(2,1)}), bf16[16,33,64,256]{3,2,1,0:T(8,128)(2,1)}, u32[]{:S(2)}, u32[]{:S(2)}) async-start(bf16[16,33,64,256]{3,2,1,0:T(8,128)(2,1)} %broadcast_select_fusion), calls=%async_computation.2 | async-start | bytes 34603008 | tf_op jit(solution)/shard_map/all_to_all | solution.py:66
  449.9 3.0 copy-start.2
